TPU v7x, 32 devices: a whole 2x2x4 slice. The times are simulated.
32 devices in a mesh: vel: 8 (over z, x), cell: 4 (over y, core).
Axes of the slice: x: 2, y: 2, z: 4, core: 2. Of those that a mesh axis runs over, the one named last changes fastest.
Arguments:
- distribution: float32 [13824, 512], P('vel', 'cell'), may hold values from 0.2 to 2
- pair_first: int32 [8, 8, 256], P('vel'), may hold values from 0 to 1727
- pair_second: int32 [8, 8, 256], P('vel'), may hold values from 0 to 1727
- pair_weight: float32 [8, 8, 256], P('vel'), may hold values from 0.05 to 0.5
- proj_pair: int32 [8, 8, 8, 64], P('vel'), may hold values from 0 to 255
- proj_target: int32 [8, 8, 8, 64], P(None, None, 'vel'), may hold values from 0 to 1727
- proj_coef: float32 [8, 8, 8, 64], P(None, None, 'vel'), may hold values from 0.1 to 1
- slot_counts: int32 [8, 8, 8], P(None, None, 'vel'), may hold values from 16 to 64, as said below
Outputs:
- transported: float32 [13824, 512], P('vel', 'cell')
- collision: float32 [13824, 512], P('vel', 'cell')
Inputs may be any that keep to these rules, and one draw needn't show every extreme that they name: slot_counts[s, p, o] live slots, counted from the first, in the list that source group s fills for partner group p and owner group o; for every offset (s - p) mod 8 one owner group gets exactly 64 live slots from every source group.
All inputs are finite; a program needn't handle non-finite values.
Results may differ from a plain program's by a relative error of at most 0.000054.
Values sent between devices are 32-bit elements; how exact they have to be, the bound alone decides.
No kernel may reach another device: no remote copies, remote signals or barrier semaphores. Data moves between devices by JAX's collectives and lax.ppermute only.
A program may use at most 64 MiB of HBM per device.

v0:
```python
import jax
import jax.numpy as jnp
from jax import lax
from jax.sharding import PartitionSpec as P

VSIDE = 24


def with_halo(cells, sides, width):
    for axis, dim in sides:
        count = lax.axis_size(axis)
        head = lax.slice_in_dim(cells, 0, width, axis=dim)
        tail = lax.slice_in_dim(cells, cells.shape[dim] - width, cells.shape[dim], axis=dim)
        cells = jnp.concatenate(
            [
                lax.ppermute(tail, axis, [(i, (i + 1) % count) for i in range(count)]),
                cells,
                lax.ppermute(head, axis, [((i + 1) % count, i) for i in range(count)]),
            ],
            axis=dim,
        )
    return cells


def on_device(
    distribution,
    pair_first,
    pair_second,
    pair_weight,
    proj_pair,
    proj_target,
    proj_coef,
    slot_counts,
):
    block_rows, cell_count = distribution.shape
    groups = lax.axis_size("vel")
    position = lax.axis_index("vel")
    slot_count = proj_target.shape[3]
    own_rows = jnp.arange(block_rows, dtype=jnp.int32)
    first_axis = (position * block_rows + own_rows) // (VSIDE * VSIDE)
    courant = ((2 * first_axis - VSIDE + 1) / (2.0 * VSIDE)).astype(jnp.float32)[:, None]
    padded = with_halo(distribution, (("cell", 1),), 1)
    transported = (
        distribution
        - jnp.maximum(courant, 0.0) * (distribution - padded[:, :-2])
        - jnp.minimum(courant, 0.0) * (padded[:, 2:] - distribution)
    )
    live_mask = (
        jnp.arange(slot_count, dtype=jnp.int32)[None, None, None, :] < slot_counts[:, :, :, None]
    )
    weights_live = jnp.where(live_mask, proj_coef, 0.0)[:, :, 0, :]
    target_rows = proj_target[:, :, 0, :]

    def pair_terms(arrived, partner):
        first_rows = pair_first[0, partner]
        product = pair_weight[0, partner][:, None] * transported[first_rows] * arrived
        one_hot = (own_rows[:, None] == first_rows[None, :]).astype(jnp.float32)
        loss_part = jnp.dot(
            one_hot, product, precision=lax.Precision.HIGHEST, preferred_element_type=jnp.float32
        )
        outgoing = product[proj_pair[0, partner]]
        return (loss_part, outgoing)

    def take_gain(received, targets_flat, factors_flat):
        one_hot = jnp.where(own_rows[:, None] == targets_flat[None, :], factors_flat[None, :], 0.0)
        return jnp.dot(
            one_hot, received, precision=lax.Precision.HIGHEST, preferred_element_type=jnp.float32
        )

    def handle(status, arrived, offset, picked=False):
        loss_sum, gain_sum, stored = status
        partner = (position - offset) % groups
        arrived = lax.dynamic_index_in_dim(arrived, partner, 0, keepdims=False)
        loss_part, outgoing = pair_terms(arrived, partner)
        loss_sum = loss_sum + loss_part
        received = lax.all_to_all(outgoing, "vel", split_axis=0, concat_axis=0, tiled=True)
        sources = jnp.arange(groups, dtype=jnp.int32)
        from_partner = (sources - offset) % groups
        factors = weights_live[sources, from_partner].reshape(-1)
        targets = target_rows[sources, from_partner].reshape(-1)
        gain_sum = gain_sum + take_gain(received.reshape(-1, cell_count), targets, factors)
        return (loss_sum, gain_sum, stored)

    stored = jnp.zeros((1,), jnp.float32)
    empty = jnp.zeros((block_rows, cell_count), jnp.float32)
    status = (empty, empty, stored)
    wanted = lax.all_to_all(pair_second, "vel", split_axis=1, concat_axis=0, tiled=True)[:, 0, :]
    picked_rows = transported[wanted]
    arrived_rows = lax.all_to_all(picked_rows, "vel", split_axis=0, concat_axis=0, tiled=True)

    def visit(offset, partial_value):
        return handle(partial_value, arrived_rows, offset, True)

    status = lax.fori_loop(0, groups, visit, status)
    loss_sum, gain_sum, stored = status
    return (transported, gain_sum - loss_sum)


def solution(mesh):
    in_specs = (
        P("vel", "cell"),
        P("vel", None, None),
        P("vel", None, None),
        P("vel", None, None),
        P("vel", None, None, None),
        P(None, None, "vel", None),
        P(None, None, "vel", None),
        P(None, None, "vel"),
    )
    out_specs = (P("vel", "cell"), P("vel", "cell"))
    return jax.shard_map(
        on_device, mesh=mesh, in_specs=in_specs, out_specs=out_specs, check_vma=False
    )
```

profile of v0, /device:TPU:0, one launch (start us, length us, event | category | flops | bytes accessed | tf_op | source)
XLA Modules:
  0.0 232.6 jit_solution(9312283286182306822)
XLA Ops:
  9.9 5.8 %all-to-all-start.1 = ((s32[1,8,256]{2,0,1:T(1,128)}), s32[1,8,256]{2,0,1:T(1,128)}, u32[]{:S(2)}, u32[]{:S(2)}) async-start(s32[1,8,256]{2,0,1:T(1,128)} %copy.16), calls=%async_computation.1 | async-start | bytes 16384 | tf_op jit(solution)/shard_map/all_to_all | solution.py:87
  17.1 5.3 %all-to-all-done.1 = s32[1,8,256]{2,0,1:T(1,128)} async-done(((s32[1,8,256]{2,0,1:T(1,128)}), s32[1,8,256]{2,0,1:T(1,128)}, u32[]{:S(2)}, u32[]{:S(2)}) %all-to-all-start.1) | async-done | bytes 8224 | tf_op jit(solution)/shard_map/all_to_all | solution.py:87
  23.1 7.6 %gather_fusion.4 = f32[2048,128]{1,0:T(8,128)} fusion(f32[1728,128]{1,0:T(8,128)S(1)} %fusion.19, s32[2048]{0:T(1024)S(1)} %broadcast_clamp_fusion), kind=kCustom, calls=%fused_computation.4 | custom fusion | bytes 2105344 | tf_op jit(solution)/shard_map/gather | solution.py:88
  30.7 3.7 %all-to-all-start.2 = ((f32[8,256,128]{2,1,0:T(8,128)}), f32[8,256,128]{2,1,0:T(8,128)S(1)}, u32[]{:S(2)}, u32[]{:S(2)}) async-start(f32[8,256,128]{2,1,0:T(8,128)} %bitcast.2), calls=%async_computation.2 | async-start | bytes 2097152 | tf_op jit(solution)/shard_map/all_to_all | solution.py:89
  34.5 23.2 %all-to-all-done.2 = f32[8,256,128]{2,1,0:T(8,128)S(1)} async-done(((f32[8,256,128]{2,1,0:T(8,128)}), f32[8,256,128]{2,1,0:T(8,128)S(1)}, u32[]{:S(2)}, u32[]{:S(2)}) %all-to-all-start.2) | async-done | bytes 1048608 | tf_op jit(solution)/shard_map/all_to_all | solution.py:89
  57.7 172.4 %while.19 = (s32[]{:T(128)}, f32[1728,128]{1,0:T(8,128)S(1)}, f32[1728,128]{1,0:T(8,128)}, s32[]{:T(128)}, s32[1,8,256]{2,1,0:T(8,128)}, /*index=5*/f32[1,8,256]...) while((s32[]{:T(128)}, f32[1728,128]{1,0:T(8,128)S(1)}, ...), condition=%wide.region_1.2_spmd.clone.clone, body=%wide.region_0.1_spmd.clone.clone.sunk | while | flops 2041598336 | bytes 5948943 | solution.py:94
  68.3 5.7 %all-to-all-done = f32[8,64,128]{2,1,0:T(8,128)S(1)} async-done(((f32[8,64,128]{2,1,0:T(8,128)}), f32[8,64,128]{2,1,0:T(8,128)S(1)}, u32[]{:S(2)}, u32[]{:S(2)}) %all-to-all-start) | async-done | bytes 262176 | tf_op jit(solution)/shard_map/while/body/eval_jaxpr/all_to_all | solution.py:76
  74.0 3.9 %fusion.40 = f32[1728,128]{1,0:T(8,128)} fusion(f32[512,128]{1,0:T(8,128)S(1)} %bitcast.48, f32[512]{0:T(512)S(1)} %broadcast_in_dim.88, s32[512]{0:T(512)S(1)} %eq.145, f32[1728,128]{1,0:T(8,128)} %get-tuple-element.477, pred[]{:T(512)S(6)} %compare.9), kind=kOutput, calls=%fused_computation.10.clone.1 | convolution fusion | flops 1361166336 | bytes 2035713 | tf_op jit(solution)/shard_map/while/body/eval_jaxpr/dot_general | solution.py:66
  88.5 6.0 %all-to-all-done = f32[8,64,128]{2,1,0:T(8,128)S(1)} async-done(((f32[8,64,128]{2,1,0:T(8,128)}), f32[8,64,128]{2,1,0:T(8,128)S(1)}, u32[]{:S(2)}, u32[]{:S(2)}) %all-to-all-start) | async-done | bytes 262176 | tf_op jit(solution)/shard_map/while/body/eval_jaxpr/all_to_all | solution.py:76
  94.5 5.0 %fusion.40 = f32[1728,128]{1,0:T(8,128)} fusion(f32[512,128]{1,0:T(8,128)S(1)} %bitcast.48, f32[512]{0:T(512)S(1)} %broadcast_in_dim.88, s32[512]{0:T(512)S(1)} %eq.145, f32[1728,128]{1,0:T(8,128)} %get-tuple-element.477, pred[]{:T(512)S(6)} %compare.9), kind=kOutput, calls=%fused_computation.10.clone.1 | convolution fusion | flops 1361166336 | bytes 2035713 | tf_op jit(solution)/shard_map/while/body/eval_jaxpr/dot_general | solution.py:66
  110.1 6.0 %all-to-all-done = f32[8,64,128]{2,1,0:T(8,128)S(1)} async-done(((f32[8,64,128]{2,1,0:T(8,128)}), f32[8,64,128]{2,1,0:T(8,128)S(1)}, u32[]{:S(2)}, u32[]{:S(2)}) %all-to-all-start) | async-done | bytes 262176 | tf_op jit(solution)/shard_map/while/body/eval_jaxpr/all_to_all | solution.py:76
  116.1 5.0 %fusion.40 = f32[1728,128]{1,0:T(8,128)} fusion(f32[512,128]{1,0:T(8,128)S(1)} %bitcast.48, f32[512]{0:T(512)S(1)} %broadcast_in_dim.88, s32[512]{0:T(512)S(1)} %eq.145, f32[1728,128]{1,0:T(8,128)} %get-tuple-element.477, pred[]{:T(512)S(6)} %compare.9), kind=kOutput, calls=%fused_computation.10.clone.1 | convolution fusion | flops 1361166336 | bytes 2035713 | tf_op jit(solution)/shard_map/while/body/eval_jaxpr/dot_general | solution.py:66
  131.9 6.0 %all-to-all-done = f32[8,64,128]{2,1,0:T(8,128)S(1)} async-done(((f32[8,64,128]{2,1,0:T(8,128)}), f32[8,64,128]{2,1,0:T(8,128)S(1)}, u32[]{:S(2)}, u32[]{:S(2)}) %all-to-all-start) | async-done | bytes 262176 | tf_op jit(solution)/shard_map/while/body/eval_jaxpr/all_to_all | solution.py:76
  137.9 5.0 %fusion.40 = f32[1728,128]{1,0:T(8,128)} fusion(f32[512,128]{1,0:T(8,128)S(1)} %bitcast.48, f32[512]{0:T(512)S(1)} %broadcast_in_dim.88, s32[512]{0:T(512)S(1)} %eq.145, f32[1728,128]{1,0:T(8,128)} %get-tuple-element.477, pred[]{:T(512)S(6)} %compare.9), kind=kOutput, calls=%fused_computation.10.clone.1 | convolution fusion | flops 1361166336 | bytes 2035713 | tf_op jit(solution)/shard_map/while/body/eval_jaxpr/dot_general | solution.py:66
  153.7 6.0 %all-to-all-done = f32[8,64,128]{2,1,0:T(8,128)S(1)} async-done(((f32[8,64,128]{2,1,0:T(8,128)}), f32[8,64,128]{2,1,0:T(8,128)S(1)}, u32[]{:S(2)}, u32[]{:S(2)}) %all-to-all-start) | async-done | bytes 262176 | tf_op jit(solution)/shard_map/while/body/eval_jaxpr/all_to_all | solution.py:76
  159.7 5.0 %fusion.40 = f32[1728,128]{1,0:T(8,128)} fusion(f32[512,128]{1,0:T(8,128)S(1)} %bitcast.48, f32[512]{0:T(512)S(1)} %broadcast_in_dim.88, s32[512]{0:T(512)S(1)} %eq.145, f32[1728,128]{1,0:T(8,128)} %get-tuple-element.477, pred[]{:T(512)S(6)} %compare.9), kind=kOutput, calls=%fused_computation.10.clone.1 | convolution fusion | flops 1361166336 | bytes 2035713 | tf_op jit(solution)/shard_map/while/body/eval_jaxpr/dot_general | solution.py:66
  169.4 3.6 %all-to-all-start = ((f32[8,64,128]{2,1,0:T(8,128)}), f32[8,64,128]{2,1,0:T(8,128)S(1)}, u32[]{:S(2)}, u32[]{:S(2)}) async-start(f32[8,64,128]{2,1,0:T(8,128)} %bitcast.46), calls=%async_computation | async-start | bytes 524288 | tf_op jit(solution)/shard_map/while/body/eval_jaxpr/all_to_all | solution.py:76
  175.5 6.0 %all-to-all-done = f32[8,64,128]{2,1,0:T(8,128)S(1)} async-done(((f32[8,64,128]{2,1,0:T(8,128)}), f32[8,64,128]{2,1,0:T(8,128)S(1)}, u32[]{:S(2)}, u32[]{:S(2)}) %all-to-all-start) | async-done | bytes 262176 | tf_op jit(solution)/shard_map/while/body/eval_jaxpr/all_to_all | solution.py:76
  181.5 5.0 %fusion.40 = f32[1728,128]{1,0:T(8,128)} fusion(f32[512,128]{1,0:T(8,128)S(1)} %bitcast.48, f32[512]{0:T(512)S(1)} %broadcast_in_dim.88, s32[512]{0:T(512)S(1)} %eq.145, f32[1728,128]{1,0:T(8,128)} %get-tuple-element.477, pred[]{:T(512)S(6)} %compare.9), kind=kOutput, calls=%fused_computation.10.clone.1 | convolution fusion | flops 1361166336 | bytes 2035713 | tf_op jit(solution)/shard_map/while/body/eval_jaxpr/dot_general | solution.py:66
  197.3 6.0 %all-to-all-done = f32[8,64,128]{2,1,0:T(8,128)S(1)} async-done(((f32[8,64,128]{2,1,0:T(8,128)}), f32[8,64,128]{2,1,0:T(8,128)S(1)}, u32[]{:S(2)}, u32[]{:S(2)}) %all-to-all-start) | async-done | bytes 262176 | tf_op jit(solution)/shard_map/while/body/eval_jaxpr/all_to_all | solution.py:76
  203.3 5.0 %fusion.40 = f32[1728,128]{1,0:T(8,128)} fusion(f32[512,128]{1,0:T(8,128)S(1)} %bitcast.48, f32[512]{0:T(512)S(1)} %broadcast_in_dim.88, s32[512]{0:T(512)S(1)} %eq.145, f32[1728,128]{1,0:T(8,128)} %get-tuple-element.477, pred[]{:T(512)S(6)} %compare.9), kind=kOutput, calls=%fused_computation.10.clone.1 | convolution fusion | flops 1361166336 | bytes 2035713 | tf_op jit(solution)/shard_map/while/body/eval_jaxpr/dot_general | solution.py:66
  213.0 3.6 %all-to-all-start = ((f32[8,64,128]{2,1,0:T(8,128)}), f32[8,64,128]{2,1,0:T(8,128)S(1)}, u32[]{:S(2)}, u32[]{:S(2)}) async-start(f32[8,64,128]{2,1,0:T(8,128)} %bitcast.46), calls=%async_computation | async-start | bytes 524288 | tf_op jit(solution)/shard_map/while/body/eval_jaxpr/all_to_all | solution.py:76
  219.1 6.0 %all-to-all-done = f32[8,64,128]{2,1,0:T(8,128)S(1)} async-done(((f32[8,64,128]{2,1,0:T(8,128)}), f32[8,64,128]{2,1,0:T(8,128)S(1)}, u32[]{:S(2)}, u32[]{:S(2)}) %all-to-all-start) | async-done | bytes 262176 | tf_op jit(solution)/shard_map/while/body/eval_jaxpr/all_to_all | solution.py:76
  225.1 5.0 %fusion.40 = f32[1728,128]{1,0:T(8,128)} fusion(f32[512,128]{1,0:T(8,128)S(1)} %bitcast.48, f32[512]{0:T(512)S(1)} %broadcast_in_dim.88, s32[512]{0:T(512)S(1)} %eq.145, f32[1728,128]{1,0:T(8,128)} %get-tuple-element.477, pred[]{:T(512)S(6)} %compare.9), kind=kOutput, calls=%fused_computation.10.clone.1 | convolution fusion | flops 1361166336 | bytes 2035713 | tf_op jit(solution)/shard_map/while/body/eval_jaxpr/dot_general | solution.py:66
  (156 shorter events, 91.9 us)
Async XLA Ops:
  2.4 3.1 %copy-start.4 = (s32[1,8,256]{2,1,0:T(8,128)S(1)}, s32[1,8,256]{2,1,0:T(8,128)}, u32[]{:S(2)}) copy-start(s32[1,8,256]{2,1,0:T(8,128)} %param.12) | copy-start | bytes 24580
  2.7 6.2 %collective-permute-start.1 = (f32[1728,1]{0,1:T(1,128)S(1)}, f32[1728,1]{0,1:T(1,128)}, u32[]{:S(2)}, u32[]{:S(2)}) collective-permute-start(f32[1728,1]{0,1:T(1,128)S(1)} %copy.19), channel_id=1, source_target_pairs={{1,0},{2,1},{3,2},{0,3},{5,4},{6,5},{7,6},{4,7},{9,8},{10,9},{11,1... | collective-permute-start | bytes 20744 | tf_op jit(solution)/shard_map/ppermute | solution.py:18
  5.5 10.3 %copy-start.1 = (f32[1728,128]{1,0:T(8,128)S(1)}, f32[1728,128]{1,0:T(8,128)}, u32[]{:S(2)}) copy-start(f32[1728,128]{1,0:T(8,128)} %param.10) | copy-start | bytes 2654212
  5.5 3.1 %collective-permute-start = (f32[1728,1]{0,1:T(1,128)S(1)}, f32[1728,1]{0,1:T(1,128)S(1)}, u32[]{:S(2)}, u32[]{:S(2)}) collective-permute-start(f32[1728,1]{0,1:T(1,128)S(1)} %copy.18), channel_id=1, source_target_pairs={{0,1},{1,2},{2,3},{3,0},{4,5},{5,6},{6,7},{7,4},{8,9},{9,10},{10,1... | collective-permute-start | bytes 20744 | tf_op jit(solution)/shard_map/ppermute | solution.py:16
  9.9 12.4 %all-to-all-start.1 = ((s32[1,8,256]{2,0,1:T(1,128)}), s32[1,8,256]{2,0,1:T(1,128)}, u32[]{:S(2)}, u32[]{:S(2)}) async-start(s32[1,8,256]{2,0,1:T(1,128)} %copy.16), calls=%async_computation.1 | async-start | bytes 16384 | tf_op jit(solution)/shard_map/all_to_all | solution.py:87
  30.7 3.7 %copy-start.3 = (f32[8,8,1,64]{3,2,1,0:T(1,128)S(1)}, f32[8,8,1,64]{3,2,1,0:T(1,128)}, u32[]{:S(2)}) copy-start(f32[8,8,1,64]{3,2,1,0:T(1,128)} %param.16) | copy-start | bytes 49156
  30.7 3.7 %copy-start.5 = (s32[8,8,1]{1,2,0:T(1,128)S(1)}, s32[8,8,1]{1,2,0:T(1,128)}, u32[]{:S(2)}) copy-start(s32[8,8,1]{1,2,0:T(1,128)} %param.17) | copy-start | bytes 772
  30.7 27.0 %copy-start.2 = (s32[8,8,1,64]{3,2,1,0:T(1,128)S(1)}, s32[8,8,1,64]{3,2,1,0:T(1,128)}, u32[]{:S(2)}) copy-start(s32[8,8,1,64]{3,2,1,0:T(1,128)} %param.15) | copy-start | bytes 49156
  30.7 27.0 %all-to-all-start.2 = ((f32[8,256,128]{2,1,0:T(8,128)}), f32[8,256,128]{2,1,0:T(8,128)S(1)}, u32[]{:S(2)}, u32[]{:S(2)}) async-start(f32[8,256,128]{2,1,0:T(8,128)} %bitcast.2), calls=%async_computation.2 | async-start | bytes 2097152 | tf_op jit(solution)/shard_map/all_to_all | solution.py:89
  62.4 11.7 %all-to-all-start = ((f32[8,64,128]{2,1,0:T(8,128)}), f32[8,64,128]{2,1,0:T(8,128)S(1)}, u32[]{:S(2)}, u32[]{:S(2)}) async-start(f32[8,64,128]{2,1,0:T(8,128)} %bitcast.46), calls=%async_computation | async-start | bytes 524288 | tf_op jit(solution)/shard_map/while/body/eval_jaxpr/all_to_all | solution.py:76
  82.6 11.9 %all-to-all-start = ((f32[8,64,128]{2,1,0:T(8,128)}), f32[8,64,128]{2,1,0:T(8,128)S(1)}, u32[]{:S(2)}, u32[]{:S(2)}) async-start(f32[8,64,128]{2,1,0:T(8,128)} %bitcast.46), calls=%async_computation | async-start | bytes 524288 | tf_op jit(solution)/shard_map/while/body/eval_jaxpr/all_to_all | solution.py:76
  104.2 12.0 %all-to-all-start = ((f32[8,64,128]{2,1,0:T(8,128)}), f32[8,64,128]{2,1,0:T(8,128)S(1)}, u32[]{:S(2)}, u32[]{:S(2)}) async-start(f32[8,64,128]{2,1,0:T(8,128)} %bitcast.46), calls=%async_computation | async-start | bytes 524288 | tf_op jit(solution)/shard_map/while/body/eval_jaxpr/all_to_all | solution.py:76
  125.8 12.1 %all-to-all-start = ((f32[8,64,128]{2,1,0:T(8,128)}), f32[8,64,128]{2,1,0:T(8,128)S(1)}, u32[]{:S(2)}, u32[]{:S(2)}) async-start(f32[8,64,128]{2,1,0:T(8,128)} %bitcast.46), calls=%async_computation | async-start | bytes 524288 | tf_op jit(solution)/shard_map/while/body/eval_jaxpr/all_to_all | solution.py:76
  147.6 12.1 %all-to-all-start = ((f32[8,64,128]{2,1,0:T(8,128)}), f32[8,64,128]{2,1,0:T(8,128)S(1)}, u32[]{:S(2)}, u32[]{:S(2)}) async-start(f32[8,64,128]{2,1,0:T(8,128)} %bitcast.46), calls=%async_computation | async-start | bytes 524288 | tf_op jit(solution)/shard_map/while/body/eval_jaxpr/all_to_all | solution.py:76
  169.4 12.1 %all-to-all-start = ((f32[8,64,128]{2,1,0:T(8,128)}), f32[8,64,128]{2,1,0:T(8,128)S(1)}, u32[]{:S(2)}, u32[]{:S(2)}) async-start(f32[8,64,128]{2,1,0:T(8,128)} %bitcast.46), calls=%async_computation | async-start | bytes 524288 | tf_op jit(solution)/shard_map/while/body/eval_jaxpr/all_to_all | solution.py:76
  191.2 12.1 %all-to-all-start = ((f32[8,64,128]{2,1,0:T(8,128)}), f32[8,64,128]{2,1,0:T(8,128)S(1)}, u32[]{:S(2)}, u32[]{:S(2)}) async-start(f32[8,64,128]{2,1,0:T(8,128)} %bitcast.46), calls=%async_computation | async-start | bytes 524288 | tf_op jit(solution)/shard_map/while/body/eval_jaxpr/all_to_all | solution.py:76
  213.0 12.1 %all-to-all-start = ((f32[8,64,128]{2,1,0:T(8,128)}), f32[8,64,128]{2,1,0:T(8,128)S(1)}, u32[]{:S(2)}, u32[]{:S(2)}) async-start(f32[8,64,128]{2,1,0:T(8,128)} %bitcast.46), calls=%async_computation | async-start | bytes 524288 | tf_op jit(solution)/shard_map/while/body/eval_jaxpr/all_to_all | solution.py:76
  230.1 2.5 %copy-start = (f32[1728,128]{1,0:T(8,128)}, f32[1728,128]{1,0:T(8,128)S(1)}, u32[]{:S(2)}) copy-start(f32[1728,128]{1,0:T(8,128)S(1)} %get-tuple-element.505) | copy-start | bytes 2654212
where the time goes:
time: 235 us; the launch traced here: 233 us
  waiting for transfers between devices  78.8 us (34%)
  matrix products  48.4 us (21%)
  local copies, waits for them, and re-layouts  47.5 us (20%)
  starting transfers between devices  40.1 us (17%)
  other arithmetic  16.9 us (7%)
    all_to_all x8, waiting for transfers between devices, handle(): lax.all_to_all(outgoing, 'vel', split_axis=0, concat_axis=0, tiled=True)  47.9 us
    dot_general x8, matrix products, take_gain(): jnp.dot(one_hot, received, precision=lax.Precision.HIGHEST, preferred_ele...  39.1 us
    all_to_all x8, starting transfers between devices, handle(): lax.all_to_all(outgoing, 'vel', split_axis=0, concat_axis=0, tiled=True)  28.1 us
    all_to_all x1, waiting for transfers between devices, on_device(): lax.all_to_all(picked_rows, 'vel', split_axis=0, concat_axis=0, tiled=True)  23.2 us
    gather x8, local copies, waits for them, and re-layouts, pair_terms(): outgoing = product[proj_pair[0, partner]]  13.2 us
    dot_general x8, matrix products, pair_terms(): jnp.dot(one_hot, product, precision=lax.Precision.HIGHEST, preferred_elem...  9.34 us
    gather x1, local copies, waits for them, and re-layouts, on_device(): picked_rows = transported[wanted]  7.61 us
    gather x8, local copies, waits for them, and re-layouts, pair_terms(): transported[first_rows]  5.83 us
  transfers between devices with their start and end apart: 12, of which 11 were waited for; matrix products, arithmetic and copies ran while one was open for 10% of the time, Pallas kernels for 0%

commit v1 on v0

v1 whole, which is shorter than its diff:
```python
import functools

import jax
import jax.numpy as jnp
from jax import lax
from jax.experimental import pallas as pl
from jax.experimental.pallas import tpu as pltpu
from jax.sharding import PartitionSpec as P

VSIDE = 24
LANE = 128
FOLD = 256
VMEM_SPEC = pl.BlockSpec(memory_space=pltpu.VMEM)


def whole_call(body, out_shape, scratch=(), name=None):
    multiple = isinstance(out_shape, (tuple, list))
    return pl.pallas_call(
        body,
        out_shape=out_shape,
        out_specs=tuple(VMEM_SPEC for _ in out_shape) if multiple else VMEM_SPEC,
        scratch_shapes=list(scratch),
        name=name,
    )


def padded_block(x, rows):
    if x.shape[0] == rows:
        return x
    return jnp.concatenate([x, jnp.zeros((rows - x.shape[0], x.shape[1]), x.dtype)], axis=0)


def flip_kernel(nodes, x_ref, y_ref, head_ref, tail_ref):
    cells, padded = y_ref.shape
    for start in range(0, padded, LANE):
        if start >= nodes:
            y_ref[:, start : start + LANE] = jnp.zeros((cells, LANE), jnp.float32)
        else:
            stop = min(start + LANE, nodes)
            y_ref[:, start : start + LANE] = padded_block(x_ref[start:stop, :], LANE).T
    head_ref[...] = y_ref[0:1, :]
    tail_ref[...] = y_ref[cells - 1 : cells, :]


def transport_kernel(x_ref, left_ref, right_ref, courant_ref, y_ref):
    x = x_ref[...]
    courant = courant_ref[...]
    left = jnp.concatenate([left_ref[...], x[:-1]], axis=0)
    right = jnp.concatenate([x[1:], right_ref[...]], axis=0)
    y_ref[...] = x - jnp.maximum(courant, 0.0) * (x - left) - jnp.minimum(courant, 0.0) * (right - x)


def unflip_kernel(nodes, x_ref, y_ref):
    for start in range(0, nodes, LANE):
        stop = min(start + LANE, nodes)
        y_ref[start:stop, :] = x_ref[:, start : start + LANE].T[: stop - start]


def scatter_rows(values, target_rows, folds):
    cells, count = values.shape
    high = values.astype(jnp.bfloat16)
    low = (values - high.astype(jnp.float32)).astype(jnp.bfloat16)
    target = jnp.concatenate(target_rows, axis=1)
    fold = jnp.floor(target * (1.0 / FOLD))
    lane = target - fold * FOLD
    fold = jnp.broadcast_to(fold, (cells, count)).astype(jnp.bfloat16)
    lane = jnp.broadcast_to(lane, (FOLD, count)).astype(jnp.bfloat16)
    index = lax.broadcasted_iota(jnp.int32, (FOLD, count), 0).astype(jnp.bfloat16)
    one_hot = jnp.where(lane == index, jnp.ones_like(lane), jnp.zeros_like(lane))
    zero = jnp.zeros_like(high)
    masks = [fold == jnp.bfloat16(f) for f in range(folds)]
    stacked = jnp.concatenate(
        [jnp.where(m, high, zero) for m in masks] + [jnp.where(m, low, zero) for m in masks], axis=0
    )
    sums = lax.dot_general(
        stacked, one_hot, (((1,), (1,)), ((), ())), preferred_element_type=jnp.float32
    )
    return sums[: folds * cells] + sums[folds * cells :]


def pick(block, lane):
    return jnp.take_along_axis(block, lane, axis=1, mode="promise_in_bounds")


def collide_kernel(groups, pairs, slots, t_ref, index_ref, out_ref, product_ref, total_ref):
    _, cells, padded = t_ref.shape
    folds = padded // FOLD
    blocks = padded // LANE
    tiles = pairs // LANE
    pair_rows = groups * tiles
    slot_rows = groups * slots // LANE
    at_second = pair_rows
    at_weight = 2 * pair_rows
    at_pair = 3 * pair_rows
    at_target = at_pair + groups * slot_rows
    at_coef = at_target + groups * slot_rows
    per_row = LANE // slots
    total_ref[...] = jnp.zeros_like(total_ref)

    def split_index(row):
        index = jnp.broadcast_to(row, (8, LANE)).astype(jnp.int32)
        return index & (LANE - 1), index // LANE

    def pick_node(group, first_cell, lane, block):
        result = None
        for b in range(blocks):
            found = pick(t_ref[group, first_cell : first_cell + 8, b * LANE : (b + 1) * LANE], lane)
            result = found if b == 0 else jnp.where(block == b, found, result)
        return result

    def from_source(source, carry):
        def with_partner(partner, carry):
            for j in range(tiles):
                row = partner * tiles + j
                first = split_index(index_ref[source, pl.ds(row, 1), :])
                second = split_index(index_ref[source, pl.ds(at_second + row, 1), :])
                weight = index_ref[source, pl.ds(at_weight + row, 1), :]
                for c in range(0, cells, 8):
                    product_ref[partner, j, c : c + 8, :] = (
                        weight * pick_node(source, c, *first) * pick_node(partner, c, *second)
                    )
            return carry

        lax.fori_loop(0, groups, with_partner, 0)

        def add_loss(half, carry):
            values, rows = [], []
            for partner in (2 * half, 2 * half + 1):
                for j in range(tiles):
                    values.append(-product_ref[partner, j])
                    rows.append(index_ref[source, pl.ds(partner * tiles + j, 1), :])
            total_ref[source] += scatter_rows(jnp.concatenate(values, axis=1), rows, folds)
            return carry

        lax.fori_loop(0, groups // 2, add_loss, 0)
        position = lax.broadcasted_iota(jnp.int32, (8, LANE), 1) // slots

        def add_gain(owner, carry):
            values, rows = [], []
            for r in range(slot_rows):
                lane, tile = split_index(index_ref[source, pl.ds(at_pair + owner * slot_rows + r, 1), :])
                coef = index_ref[owner, pl.ds(at_coef + source * slot_rows + r, 1), :]
                column = []
                for c in range(0, cells, 8):
                    result = None
                    for q in range(per_row):
                        for j in range(tiles):
                            found = pick(product_ref[r * per_row + q, j, c : c + 8, :], lane)
                            mine = (tile == j) & (position == q)
                            result = found if result is None else jnp.where(mine, found, result)
                    column.append(result * coef)
                values.append(jnp.concatenate(column, axis=0))
                rows.append(index_ref[owner, pl.ds(at_target + source * slot_rows + r, 1), :])
            total_ref[owner] += scatter_rows(jnp.concatenate(values, axis=1), rows, folds)
            return carry

        lax.fori_loop(0, groups, add_gain, 0)
        return carry

    lax.fori_loop(0, groups, from_source, 0)
    for owner in range(groups):
        for f in range(folds):
            out_ref[owner, :, f * FOLD : (f + 1) * FOLD] = total_ref[
                owner, f * cells : (f + 1) * cells, :
            ]


def on_device(
    distribution,
    pair_first,
    pair_second,
    pair_weight,
    proj_pair,
    proj_target,
    proj_coef,
    slot_counts,
):
    nodes, cells = distribution.shape
    groups = lax.axis_size("vel")
    position = lax.axis_index("vel")
    pairs = pair_first.shape[2]
    slots = proj_target.shape[3]
    padded = -(-nodes // FOLD) * FOLD
    part = cells // groups
    f32 = jnp.float32

    live = jnp.arange(slots, dtype=jnp.int32) < slot_counts[:, :, :, None]
    coef = jnp.where(live, proj_coef, 0.0)
    table = jnp.concatenate(
        [
            pair_first.reshape(-1, LANE).astype(f32),
            pair_second.reshape(-1, LANE).astype(f32),
            pair_weight.reshape(-1, LANE),
            proj_pair[0].transpose(1, 0, 2).reshape(-1, LANE).astype(f32),
            proj_target.reshape(-1, LANE).astype(f32),
            coef.reshape(-1, LANE),
        ],
        axis=0,
    )
    tables = lax.all_to_all(
        jnp.broadcast_to(table[None], (groups,) + table.shape), "vel", 0, 0, tiled=True
    )

    node = position * nodes + jnp.arange(padded, dtype=jnp.int32)
    courant = ((2 * (node // (VSIDE * VSIDE)) - VSIDE + 1) / (2.0 * VSIDE)).astype(f32)[None, :]
    edge = jax.ShapeDtypeStruct((1, padded), f32)
    flat = jax.ShapeDtypeStruct((cells, padded), f32)
    turned, head, tail = whole_call(
        functools.partial(flip_kernel, nodes), (flat, edge, edge), name="flip"
    )(distribution)
    count = lax.axis_size("cell")
    left = lax.ppermute(tail, "cell", [(i, (i + 1) % count) for i in range(count)])
    right = lax.ppermute(head, "cell", [((i + 1) % count, i) for i in range(count)])
    moved = whole_call(transport_kernel, flat, name="transport")(turned, left, right, courant)
    back = whole_call(
        functools.partial(unflip_kernel, nodes), jax.ShapeDtypeStruct((nodes, cells), f32), name="unflip"
    )
    everywhere = lax.all_to_all(moved.reshape(groups, part, padded), "vel", 0, 0, tiled=True)
    transported = back(moved)
    change = whole_call(
        functools.partial(collide_kernel, groups, pairs, slots),
        jax.ShapeDtypeStruct((groups, part, padded), f32),
        scratch=[
            pltpu.VMEM((groups, pairs // LANE, part, LANE), f32),
            pltpu.VMEM((groups, padded // FOLD * part, FOLD), f32),
        ],
        name="collide",
    )(everywhere, tables)
    owned = lax.all_to_all(change, "vel", 0, 0, tiled=True)
    collision = back(owned.reshape(cells, padded))
    return transported, collision


def solution(mesh):
    in_specs = (
        P("vel", "cell"),
        P("vel", None, None),
        P("vel", None, None),
        P("vel", None, None),
        P("vel", None, None, None),
        P(None, None, "vel", None),
        P(None, None, "vel", None),
        P(None, None, "vel"),
    )
    out_specs = (P("vel", "cell"), P("vel", "cell"))
    return jax.shard_map(
        on_device, mesh=mesh, in_specs=in_specs, out_specs=out_specs, check_vma=False
    )
```

time: 235 us -> 131 us (0.56)
  Pallas kernels: 0 us -> 55.5 us
  waiting for transfers between devices: 78.8 us -> 28 us
  matrix products: 48.4 us -> 0 us
  local copies, waits for them, and re-layouts: 47.5 us -> 4.69 us
  starting transfers between devices: 40.1 us -> 12.6 us
  blocking collectives: 0 us -> 27.2 us
  other arithmetic: 16.9 us -> 1.6 us
    pallas_call x0 -> x5, Pallas kernels: none -> 55.5 us  [the longest x1 45.8 us: on_device(): whole_call(functools.partial(collide_kernel, groups, pairs, slots), jax.S...]
    all_to_all x10 -> x2, waiting for transfers between devices: 76.4 us -> 27.1 us  [the longest x1 20.1 us: on_device(): owned = lax.all_to_all(change, 'vel', 0, 0, tiled=True)]
    dot_general x16 -> x0, matrix products: 48.4 us -> none  [the longest x8 39.1 us: take_gain(): jnp.dot(one_hot, received, precision=lax.Precision.HIGHEST, preferred_ele...]
    gather x33 -> x0, local copies, waits for them, and re-layouts: 35.7 us -> none  [the longest x8 13.2 us: pair_terms(): outgoing = product[proj_pair[0, partner]]]
    all_to_all x0 -> x1, blocking collectives: none -> 27.2 us  [on_device(): lax.all_to_all(moved.reshape(groups, part, padded), 'vel', 0, 0, tiled=True)]
    all_to_all x10 -> x2, starting transfers between devices: 37.6 us -> 10.8 us  [the longest x1 7.28 us: on_device(): lax.all_to_all(jnp.broadcast_to(table[None], (groups,) + table.shape), 'v...]
    select_n x17 -> x1, other arithmetic: 11.9 us -> 0.25 us  [on_device(): coef = jnp.where(live, proj_coef, 0.0)]
    dynamic_slice x8 -> x0, local copies, waits for them, and re-layouts: 5.61 us -> none  [pair_terms(): pair_weight[0, partner][:, None] * transported[first_rows] * arrived]
  transfers between devices with their start and end apart: 12 -> 4, of which waited for: 11 -> 3; matrix products, arithmetic and copies ran while one was open for 10% -> 0% of each run, Pallas kernels for 0% -> 6%
where the time goes in v1:
time: 131 us; the launch traced here: 130 us
  Pallas kernels  55.5 us (42%)
  waiting for transfers between devices  28 us (21%)
  blocking collectives  27.2 us (21%)
  starting transfers between devices  12.6 us (10%)
  local copies, waits for them, and re-layouts  4.69 us (4%)
  other arithmetic  1.6 us (1%)
    pallas_call x1, Pallas kernels, on_device(): whole_call(functools.partial(collide_kernel, groups, pairs, slots), jax.S...  45.8 us
    all_to_all x1, blocking collectives, on_device(): lax.all_to_all(moved.reshape(groups, part, padded), 'vel', 0, 0, tiled=True)  27.2 us
    all_to_all x1, waiting for transfers between devices, on_device(): owned = lax.all_to_all(change, 'vel', 0, 0, tiled=True)  20.1 us
    all_to_all x1, starting transfers between devices, on_device(): lax.all_to_all(jnp.broadcast_to(table[None], (groups,) + table.shape), 'v...  7.28 us
    all_to_all x1, waiting for transfers between devices, on_device(): lax.all_to_all(jnp.broadcast_to(table[None], (groups,) + table.shape), 'v...  7.05 us
    unnamed x25, local copies, waits for them, and re-layouts  3.6 us
    all_to_all x1, starting transfers between devices, on_device(): owned = lax.all_to_all(change, 'vel', 0, 0, tiled=True)  3.55 us
  transfers between devices with their start and end apart: 4, of which 3 were waited for; matrix products, arithmetic and copies ran while one was open for 0% of the time, Pallas kernels for 6%

profile of v1, /device:TPU:0, one launch (start us, length us, event | category | flops | bytes accessed | tf_op | source)
XLA Modules:
  0.0 130.3 jit_solution(1060972635072164108)
XLA Ops:
  0.6 0.7 convert_element_type.41
  1.3 0.7 copy-done.5
  2.0 0.7 copy-done.6
  2.8 0.1 convert_element_type.48
  2.9 0.6 copy-done.4
  3.5 0.2 fusion
  3.8 0.1 convert_element_type.50
  3.9 0.1 reshape.82
  4.0 0.9 broadcast_in_dim.7
  4.8 7.3 %all-to-all-start.1 = ((f32[8,144,128]{2,1,0:T(8,128)}), f32[8,144,128]{2,1,0:T(8,128)S(1)}, u32[]{:S(2)}, u32[]{:S(2)}) async-start(f32[8,144,128]{2,1,0:T(8,128)} %broadcast_in_dim.7), calls=%async_computation.1 | async-start | bytes 1179648 | tf_op jit(solution)/shard_map/all_to_all | solution.py:200
  12.1 2.5 %flip.1 = (f32[128,1792]{1,0:T(8,128)}, f32[1,1792]{1,0:T(1,128)}, f32[1,1792]{1,0:T(1,128)}) custom-call(f32[1728,128]{1,0:T(8,128)} %x_ref.1), custom_call_target="tpu_custom_call" | custom-call | tf_op jit(solution)/shard_map/flip/pallas_call | solution.py:208
  14.6 1.7 %collective-permute-start.1 = (f32[1,1792]{1,0:T(1,128)}, f32[1,1792]{1,0:T(1,128)S(1)}, u32[]{:S(2)}, u32[]{:S(2)}) collective-permute-start(f32[1,1792]{1,0:T(1,128)} %get-tuple-element.7), channel_id=1, source_target_pairs={{1,0},{2,1},{3,2},{0,3},{5,4},{6,5},{7,6},{4,7},{9,8},{10,9},{11,1... | collective-permute-start | bytes 21512 | tf_op jit(solution)/shard_map/ppermute | solution.py:213
  16.3 0.7 convert_multiply_fusion.courant_ref
  17.0 0.9 collective-permute-done.left_ref
  17.9 0.6 copy-done.7
  18.5 2.5 %transport.1.x_ref = f32[128,1792]{1,0:T(8,128)} custom-call(f32[128,1792]{1,0:T(8,128)} %get-tuple-element.5.x_ref, f32[1,1792]{1,0:T(1,128)} %copy-done.7, f32[1,1792]{1,0:T(1,128)} %copy-done.8, f32[1,1792]{1,0:T(1,128)} %convert_multiply_fusion.courant_ref), custom_call_target="tpu_custom_call" | custom-call | tf_op jit(solution)/shard_map/transport/pallas_call | solution.py:214
  20.9 7.0 %all-to-all-done.1.index_ref = f32[8,144,128]{2,1,0:T(8,128)S(1)} async-done(((f32[8,144,128]{2,1,0:T(8,128)}), f32[8,144,128]{2,1,0:T(8,128)S(1)}, u32[]{:S(2)}, u32[]{:S(2)}) %all-to-all-start.1) | async-done | bytes 589856 | tf_op jit(solution)/shard_map/all_to_all | solution.py:200
  28.0 27.2 %all_to_all.15.t_ref = f32[8,16,1792]{2,1,0:T(8,128)} all-to-all(f32[8,16,1792]{2,1,0:T(8,128)} %bitcast.7), channel_id=1, replica_groups=mesh['vel'=8,'cell'=4] {'vel'}, dimensions={0} | all-to-all | bytes 1835008 | tf_op jit(solution)/shard_map/all_to_all | solution.py:218
  55.2 45.8 %collide.1 = f32[8,16,1792]{2,1,0:T(8,128)} custom-call(f32[8,16,1792]{2,1,0:T(8,128)} %all_to_all.15.t_ref, f32[8,144,128]{2,1,0:T(8,128)} %copy-done.1), custom_call_target="tpu_custom_call" | custom-call | tf_op jit(solution)/shard_map/collide/pallas_call | solution.py:220
  101.0 3.6 %all-to-all-start.2 = ((f32[8,16,1792]{2,1,0:T(8,128)}), f32[8,16,1792]{2,1,0:T(8,128)S(1)}, u32[]{:S(2)}, u32[]{:S(2)}) async-start(f32[8,16,1792]{2,1,0:T(8,128)} %collide.1), calls=%async_computation.2 | async-start | bytes 1835008 | tf_op jit(solution)/shard_map/all_to_all | solution.py:229
  104.6 2.4 %unflip.2 = f32[1728,128]{1,0:T(8,128)} custom-call(f32[128,1792]{1,0:T(8,128)} %transport.1.x_ref), custom_call_target="tpu_custom_call" | custom-call | tf_op jit(solution)/shard_map/unflip/pallas_call | solution.py:219
  107.0 20.1 %all-to-all-done.2 = f32[8,16,1792]{2,1,0:T(8,128)S(1)} async-done(((f32[8,16,1792]{2,1,0:T(8,128)}), f32[8,16,1792]{2,1,0:T(8,128)S(1)}, u32[]{:S(2)}, u32[]{:S(2)}) %all-to-all-start.2) | async-done | bytes 917536 | tf_op jit(solution)/shard_map/all_to_all | solution.py:229
  127.0 0.9 copy-done
  128.0 2.4 %unflip.3 = f32[1728,128]{1,0:T(8,128)} custom-call(f32[128,1792]{1,0:T(8,128)} %bitcast.8), custom_call_target="tpu_custom_call" | custom-call | tf_op jit(solution)/shard_map/unflip/pallas_call | solution.py:230
  (29 shorter events, 0.2 us)
Async XLA Ops:
  1.3 0.7 copy-start.5
  1.3 1.4 %copy-start.2 = (s32[1,8,8,64]{3,2,1,0:T(8,128)S(1)}, s32[1,8,8,64]{3,2,1,0:T(8,128)}, u32[]{:S(2)}) copy-start(s32[1,8,8,64]{3,2,1,0:T(8,128)} %param.12) | copy-start | bytes 49156
  2.0 0.7 copy-start.6
  2.7 0.8 copy-start.4
  2.8 0.8 copy-start.3
  2.8 0.8 copy-start.9
  4.8 23.2 %all-to-all-start.1 = ((f32[8,144,128]{2,1,0:T(8,128)}), f32[8,144,128]{2,1,0:T(8,128)S(1)}, u32[]{:S(2)}, u32[]{:S(2)}) async-start(f32[8,144,128]{2,1,0:T(8,128)} %broadcast_in_dim.7), calls=%async_computation.1 | async-start | bytes 1179648 | tf_op jit(solution)/shard_map/all_to_all | solution.py:200
  14.6 3.3 %collective-permute-start = (f32[1,1792]{1,0:T(1,128)}, f32[1,1792]{1,0:T(1,128)S(1)}, u32[]{:S(2)}, u32[]{:S(2)}) collective-permute-start(f32[1,1792]{1,0:T(1,128)} %get-tuple-element.6), channel_id=1, source_target_pairs={{0,1},{1,2},{2,3},{3,0},{4,5},{5,6},{6,7},{7,4},{8,9},{9,10},{10,1... | collective-permute-start | bytes 21512 | tf_op jit(solution)/shard_map/ppermute | solution.py:212
  14.6 3.3 %collective-permute-start.1 = (f32[1,1792]{1,0:T(1,128)}, f32[1,1792]{1,0:T(1,128)S(1)}, u32[]{:S(2)}, u32[]{:S(2)}) collective-permute-start(f32[1,1792]{1,0:T(1,128)} %get-tuple-element.7), channel_id=1, source_target_pairs={{1,0},{2,1},{3,2},{0,3},{5,4},{6,5},{7,6},{4,7},{9,8},{10,9},{11,1... | collective-permute-start | bytes 21512 | tf_op jit(solution)/shard_map/ppermute | solution.py:213
  17.8 0.6 copy-start.7
  17.9 0.6 copy-start.8
  28.0 27.3 %copy-start.1 = (f32[8,144,128]{2,1,0:T(8,128)}, f32[8,144,128]{2,1,0:T(8,128)S(1)}, u32[]{:S(2)}) copy-start(f32[8,144,128]{2,1,0:T(8,128)S(1)} %all-to-all-done.1.index_ref) | copy-start | bytes 1769476
  101.0 26.0 %all-to-all-start.2 = ((f32[8,16,1792]{2,1,0:T(8,128)}), f32[8,16,1792]{2,1,0:T(8,128)S(1)}, u32[]{:S(2)}, u32[]{:S(2)}) async-start(f32[8,16,1792]{2,1,0:T(8,128)} %collide.1), calls=%async_computation.2 | async-start | bytes 1835008 | tf_op jit(solution)/shard_map/all_to_all | solution.py:229
  127.0 0.9 copy-start
